TPU v7x, 256 devices: a whole 4x4x8 slice. The times are simulated.
256 devices in a mesh: shard: 16 (over y, z_hi, core), rep: 16 (over x, z_lo).
Axes of the slice: x: 4, y: 4, z: 8 (z_hi: 2, z_lo: 4; z = z_hi * 4 + z_lo), core: 2. Of those that a mesh axis runs over, the one named last changes fastest.
Arguments:
- inputs: bfloat16 [50432, 768], P(('shard', 'rep')), may hold values from -6 to 6
- norm1_gain: float32 [768], replicated, may hold values from 0.25 to 1.75
- w_qkv: bfloat16 [768, 2304], P('shard'), may hold values from -0.21875 to 0.21875
- w_proj: bfloat16 [768, 768], P('shard'), may hold values from -0.875 to 0.875
- norm2_gain: float32 [768], replicated, may hold values from 0.25 to 1.75
- w_router: bfloat16 [768, 32], P('shard'), may hold values from -0.21875 to 0.21875
- w_expert_in: bfloat16 [2, 768, 3072], P(None, 'shard'), may hold values from -0.21875 to 0.21875
- w_expert_out: bfloat16 [2, 3072, 768], P(None, 'shard'), may hold values from -0.875 to 0.875
- expert_ids: int32 [50432, 2], P(('shard', 'rep')), may hold values from 0 to 1, all different within a row
- capacity: int32 [2], replicated, may hold values from 64 to 128, as said below
- cotangent: bfloat16 [50432, 768], P(('shard', 'rep')), may hold values from -6 to 6
Outputs:
- outputs: bfloat16 [50432, 768], P(('shard', 'rep'))
- grad_inputs: float32 [50432, 768], P(('shard', 'rep'))
- grad_norm1_gain: float32 [768], replicated
- grad_qkv: float32 [768, 2304], P('shard')
- grad_proj: float32 [768, 768], P('shard')
- grad_norm2_gain: float32 [768], replicated
- grad_router: float32 [768, 32], P('shard')
- grad_expert_in: float32 [2, 768, 3072], P(None, 'shard')
- grad_expert_out: float32 [2, 3072, 768], P(None, 'shard')
Inputs may be any that keep to these rules, and one draw needn't show every extreme that they name: Every expert's capacity is 64 to 128; some expert has exactly 128. `expert_ids`: the two experts of a token differ.
All inputs are finite; a program needn't handle non-finite values.
Results may differ from a plain program's by a relative error of at most 0.025.
Values may be sent and summed in bfloat16 or wider, within the bound.
No kernel may reach another device: no remote copies, remote signals or barrier semaphores. Data moves between devices by JAX's collectives and lax.ppermute only.
A program may use at most 128 MiB of HBM per device.

v0:
```python
import jax
import jax.numpy as jnp
from jax import lax
from jax.sharding import PartitionSpec as P

HEADS = 12
HD = 64
EXPERTS = 32
E_WIN = 2
SEQ = 197
CAP = 128
EPS = 1e-06


def layer_norm(values, gain):
    centred = values - jnp.mean(values, axis=-1, keepdims=True)
    inverse = lax.rsqrt(jnp.mean(centred * centred, axis=-1, keepdims=True) + EPS)
    normed = centred * inverse
    return (normed, inverse, (normed * gain).astype(jnp.bfloat16))


def layer_norm_back(grad_out, normed, inverse, gain):
    scaled = grad_out * gain
    grad_in = inverse * (
        scaled
        - jnp.mean(scaled, axis=-1, keepdims=True)
        - normed * jnp.mean(scaled * normed, axis=-1, keepdims=True)
    )
    return (grad_in, jnp.sum(grad_out * normed, axis=0))


def butterfly_sum(value, axis, size, wire=None):
    step = 1
    while step < size:
        pairs = [(i, i ^ step) for i in range(size)]
        sent = value if wire is None else value.astype(wire)
        other = lax.ppermute(sent, axis, pairs)
        value = sent.astype(jnp.float32) + other.astype(jnp.float32)
        step *= 2
    return value


def heads_view(block, images):
    return block.reshape(images, SEQ, HEADS, HD)


def attention_scores(qkv, images):
    width = HEADS * HD
    query = heads_view(qkv[:, :width], images)
    keys = heads_view(qkv[:, width : 2 * width], images)
    values = heads_view(qkv[:, 2 * width :], images)
    scores = jnp.einsum(
        "bqhd,bkhd->bhqk", query, keys, preferred_element_type=jnp.float32
    ) * HD ** (-0.5)
    return (query, keys, values, scores)


def attention_forward(qkv, images):
    query, keys, values, scores = attention_scores(qkv, images)
    logsum = jax.nn.logsumexp(scores, axis=-1, keepdims=True)
    probs = jnp.exp(scores - logsum).astype(jnp.bfloat16)
    mixed = jnp.einsum("bhqk,bkhd->bqhd", probs, values, preferred_element_type=jnp.float32).astype(
        jnp.bfloat16
    )
    return (mixed.reshape(images * SEQ, HEADS * HD), logsum)


def attention_backward(qkv, mixed, logsum, grad_mixed, images):
    query, keys, values, scores = attention_scores(qkv, images)
    probs_full = jnp.exp(scores - logsum)
    probs = probs_full.astype(jnp.bfloat16)
    grad_out = heads_view(grad_mixed, images)
    out_rows = heads_view(mixed, images)
    grad_values = jnp.einsum("bhqk,bqhd->bkhd", probs, grad_out, preferred_element_type=jnp.float32)
    grad_probs = jnp.einsum("bqhd,bkhd->bhqk", grad_out, values, preferred_element_type=jnp.float32)
    delta = jnp.sum(grad_out.astype(jnp.float32) * out_rows.astype(jnp.float32), axis=-1)
    delta = jnp.transpose(delta, (0, 2, 1))[..., None]
    grad_scores = (probs_full * (grad_probs - delta)).astype(jnp.bfloat16)
    scale = HD ** (-0.5)
    grad_query = (
        jnp.einsum("bhqk,bkhd->bqhd", grad_scores, keys, preferred_element_type=jnp.float32) * scale
    )
    grad_keys = (
        jnp.einsum("bhqk,bqhd->bkhd", grad_scores, query, preferred_element_type=jnp.float32)
        * scale
    )
    width = HEADS * HD
    rows = images * SEQ
    return jnp.concatenate(
        [
            grad_query.reshape(rows, width),
            grad_keys.reshape(rows, width),
            grad_values.reshape(rows, width),
        ],
        axis=1,
    ).astype(jnp.bfloat16)


def route_masks(expert_ids, capacity):
    count = expert_ids.shape[0]
    picked_hot = (expert_ids[:, :, None] == jnp.arange(E_WIN)[None, None, :]).astype(jnp.int32)
    ordered = jnp.transpose(picked_hot, (1, 0, 2)).reshape(2 * count, E_WIN)
    before = jnp.cumsum(ordered, axis=0) - ordered
    position = jnp.sum(before * ordered, axis=1).reshape(2, count).T
    limit = jnp.sum(picked_hot * capacity[None, None, :], axis=2)
    kept_mask = (position < limit).astype(jnp.float32)
    slot_hot = (position[:, :, None] == jnp.arange(CAP)[None, None, :]).astype(jnp.float32)
    return (
        kept_mask[:, :, None, None]
        * picked_hot.astype(jnp.float32)[:, :, :, None]
        * slot_hot[:, :, None, :]
    )


def body(
    inputs,
    norm1_gain,
    w_qkv,
    w_proj,
    norm2_gain,
    w_router,
    w_expert_in,
    w_expert_out,
    expert_ids,
    capacity,
    cotangent,
):
    high = lax.Precision.HIGHEST
    images = inputs.shape[0] // SEQ
    shard_rows = w_qkv.shape[0]
    hid_rows = w_expert_out.shape[1]
    width = HEADS * HD
    dense_all = lax.all_gather(
        jnp.concatenate([w_qkv, w_proj, w_router], axis=1), "shard", axis=0, tiled=True
    )
    full_qkv, full_proj, full_router = (
        dense_all[:, : 3 * width],
        dense_all[:, 3 * width : 4 * width],
        dense_all[:, 4 * width :],
    )
    x_float = inputs.astype(jnp.float32)
    normed1, inverse1, hidden1 = layer_norm(x_float, norm1_gain)
    qkv = jnp.dot(hidden1, full_qkv, preferred_element_type=jnp.float32).astype(jnp.bfloat16)
    mixed, logsum = attention_forward(qkv, images)
    attended = x_float + jnp.dot(mixed, full_proj, preferred_element_type=jnp.float32)
    normed2, inverse2, hidden2 = layer_norm(attended, norm2_gain)
    logits = jnp.dot(hidden2, full_router, preferred_element_type=jnp.float32)
    router = jax.nn.softmax(logits, axis=-1)
    expert_hot = (expert_ids[:, :, None] == jnp.arange(EXPERTS)[None, None, :]).astype(jnp.float32)
    gate = jnp.sum(router[:, None, :] * expert_hot, axis=2)
    masks = route_masks(expert_ids, capacity)
    dispatch_float = jnp.sum(masks, axis=1)
    dispatch = dispatch_float.astype(jnp.bfloat16)
    combine = jnp.sum(masks * gate[:, :, None, None], axis=1)
    expert_rows = jnp.einsum(
        "rec,rd->ecd", dispatch, hidden2, preferred_element_type=jnp.float32
    ).astype(jnp.bfloat16)
    w_in_cols = lax.all_to_all(w_expert_in, "shard", 2, 1, tiled=True)
    grad = cotangent.astype(jnp.float32)
    grad_eout = jnp.einsum("rec,rd->ecd", combine, grad, precision=high).astype(jnp.bfloat16)
    gathered = lax.all_gather(jnp.stack([expert_rows, grad_eout]), "shard", axis=2, tiled=True)
    rows_all, geout_all = (gathered[0], gathered[1])
    pre = jnp.einsum("erd,edh->erh", rows_all, w_in_cols, preferred_element_type=jnp.float32)
    activated = jax.nn.gelu(pre, approximate=False).astype(jnp.bfloat16)
    out_part = jnp.einsum(
        "erh,ehd->erd", activated, w_expert_out, preferred_element_type=jnp.float32
    ).astype(jnp.bfloat16)
    grad_act = jnp.einsum(
        "erd,ehd->erh", geout_all, w_expert_out, preferred_element_type=jnp.float32
    )
    slope = (
        0.5 * (1.0 + jax.scipy.special.erf(pre * 0.7071067811865476))
        + pre * jnp.exp(-0.5 * pre * pre) * 0.3989422804014327
    )
    grad_pre = (grad_act * slope).astype(jnp.bfloat16)
    rows_part = jnp.einsum(
        "erh,edh->erd", grad_pre, w_in_cols, preferred_element_type=jnp.float32
    ).astype(jnp.bfloat16)
    scattered = lax.psum_scatter(
        jnp.stack([out_part, rows_part]), "shard", scatter_dimension=2, tiled=True
    )
    expert_out, grad_rows = (scattered[0], scattered[1])
    eout_float = expert_out.astype(jnp.float32)
    moe = jnp.einsum("rec,ecd->rd", combine, eout_float, precision=high)
    outputs = (attended + moe).astype(jnp.bfloat16)
    matched = jnp.einsum("rd,ecd->rec", grad, eout_float, precision=high)
    grad_gate = jnp.sum(masks * matched[:, None, :, :], axis=(2, 3))
    back_qkv, back_proj, back_router = (full_qkv, full_proj, full_router)
    gin_cols = jnp.einsum("erd,erh->edh", rows_all, grad_pre, preferred_element_type=jnp.float32)
    gin_local = lax.all_to_all(gin_cols.astype(jnp.bfloat16), "shard", 1, 2, tiled=True)
    gout_local = jnp.einsum(
        "erh,erd->ehd", activated, geout_all, preferred_element_type=jnp.float32
    ).astype(jnp.bfloat16)
    grad_probs = jnp.sum(grad_gate[:, :, None] * expert_hot, axis=1)
    grad_logits = (
        router * (grad_probs - jnp.sum(router * grad_probs, axis=-1, keepdims=True))
    ).astype(jnp.bfloat16)
    grad_hidden2 = jnp.einsum(
        "rec,ecd->rd", dispatch, grad_rows, preferred_element_type=jnp.float32
    ) + jnp.einsum("re,de->rd", grad_logits, back_router, preferred_element_type=jnp.float32)
    grad_norm2, gain2 = layer_norm_back(grad_hidden2, normed2, inverse2, norm2_gain)
    grad_attended = grad + grad_norm2
    grad_branch = grad_attended.astype(jnp.bfloat16)
    grad_mixed = jnp.einsum(
        "rk,dk->rd", grad_branch, back_proj, preferred_element_type=jnp.float32
    ).astype(jnp.bfloat16)
    grad_qkv_rows = attention_backward(qkv, mixed, logsum, grad_mixed, images)
    grad_hidden1 = jnp.einsum(
        "rk,dk->rd", grad_qkv_rows, back_qkv, preferred_element_type=jnp.float32
    )
    grad_norm1, gain1 = layer_norm_back(grad_hidden1, normed1, inverse1, norm1_gain)
    grad_inputs = grad_attended + grad_norm1
    n_shard = lax.axis_size("shard")
    n_rep = lax.axis_size("rep")
    gains = butterfly_sum(jnp.stack([gain1, gain2]), "shard", n_shard)
    gains = butterfly_sum(gains, "rep", n_rep)
    gain1_total, gain2_total = (gains[0], gains[1])
    dense_local = lax.psum_scatter(
        jnp.concatenate(
            [
                jnp.einsum("rc,rk->ck", hidden1, grad_qkv_rows, preferred_element_type=jnp.float32),
                jnp.einsum("rc,rk->ck", mixed, grad_branch, preferred_element_type=jnp.float32),
                jnp.einsum("rc,rk->ck", hidden2, grad_logits, preferred_element_type=jnp.float32),
            ],
            axis=1,
        ).astype(jnp.bfloat16),
        "shard",
        scatter_dimension=0,
        tiled=True,
    )
    dense_total, in_total, out_total = (
        butterfly_sum(dense_local, "rep", n_rep, jnp.bfloat16),
        butterfly_sum(gin_local, "rep", n_rep, jnp.bfloat16),
        butterfly_sum(gout_local, "rep", n_rep, jnp.bfloat16),
    )
    return (
        outputs,
        grad_inputs,
        gain1_total,
        dense_total[:, : 3 * width],
        dense_total[:, 3 * width : 4 * width],
        gain2_total,
        dense_total[:, 4 * width :],
        in_total,
        out_total,
    )


def solution(mesh):
    in_specs = (
        P(("shard", "rep"), None),
        P(),
        P("shard", None),
        P("shard", None),
        P(),
        P("shard", None),
        P(None, "shard", None),
        P(None, "shard", None),
        P(("shard", "rep"), None),
        P(),
        P(("shard", "rep"), None),
    )
    out_specs = (
        P(("shard", "rep"), None),
        P(("shard", "rep"), None),
        P(),
        P("shard", None),
        P("shard", None),
        P(),
        P("shard", None),
        P(None, "shard", None),
        P(None, "shard", None),
    )
    return jax.shard_map(body, mesh=mesh, in_specs=in_specs, out_specs=out_specs, check_vma=False)
```

profile of v0, /device:TPU:4, one launch (start us, length us, event | category | flops | bytes accessed | tf_op | source)
XLA Modules:
  0.0 680.0 jit_solution(1901787044144280053)
XLA Ops:
  17.6 79.0 %all-gather.3.cloned.1.call-done = bf16[768,3104]{1,0:T(8,128)(2,1)} async-done(((bf16[48,3104]{1,0:T(8,128)(2,1)}), bf16[768,3104]{1,0:T(8,128)(2,1)}) %all-gather.3.cloned.1.call-update) | async-done | bytes 4767760 | tf_op jit(solution)/shard_map/all_gather | solution.py:133
  115.4 4.3 copy.162
  119.7 4.1 reshape.249
  123.9 39.2 %all_to_all.36 = bf16[16,2,9216]{2,1,0:T(2,128)(2,1)} all-to-all(bf16[16,2,9216]{2,1,0:T(2,128)(2,1)} %reshape.249), channel_id=1, replica_groups=mesh['shard'=16,'rep'=16] {'shard'}, dimensions={0} | all-to-all | bytes 1179648 | tf_op jit(solution)/shard_map/all_to_all | solution.py:158
  166.4 4.7 copy.163
  171.1 93.5 %all-gather.5.cloned.1.call-done = bf16[2,2,2048,768]{3,2,1,0:T(8,128)(2,1)} async-done(((bf16[2,2,128,768]{3,2,1,0:T(8,128)(2,1)}), bf16[2,2,2048,768]{3,2,1,0:T(8,128)(2,1)}) %all-gather.5.cloned.1.call-update) | async-done | bytes 12582928 | tf_op jit(solution)/shard_map/all_gather | solution.py:161
  264.6 5.5 fusion.34
  270.2 4.6 fusion.12
  277.0 7.2 %fusion.6 = bf16[2,2048,192]{1,2,0:T(8,128)(2,1)S(1)} fusion(f32[2,2048,192]{1,2,0:T(8,128)S(1)} %get-tuple-element.84, u8[2048,192]{0,1:T(8,128)(4,1)S(1)} %get-tuple-element.64, u8[2048,192]{0,1:T(8,128)(4,1)S(1)} %get-tuple-element.63), kind=kLoop, calls=%fused_computation.16 | loop fusion | flops 55050240 | bytes 5505024 | tf_op jit(solution)/shard_map/convert_element_type | solution.py:164
  286.1 5.6 pad_maximum_fusion
  292.0 170.9 %reduce-scatter.3.cloned.1.call-done = bf16[2,2,128,768]{3,2,1,0:T(8,128)(2,1)} async-done(((bf16[2,2,2048,768]{3,2,1,0:T(8,128)(2,1)}), bf16[2,2,128,768]{3,2,1,0:T(8,128)(2,1)}) %reduce-scatter.3.cloned.1.call-update) | async-done | bytes 786448 | tf_op jit(solution)/shard_map/reduce_scatter | solution.py:179
  488.1 4.3 fusion.23
  493.9 4.5 fusion.24
  500.2 3.6 all-to-all-start.1
  508.5 20.7 %all-to-all-done.1 = bf16[2,768,192]{2,0,1:T(2,128)(2,1)S(1)} async-done(((bf16[2,768,192]{2,0,1:T(2,128)(2,1)}), bf16[2,768,192]{2,0,1:T(2,128)(2,1)S(1)}, u32[]{:S(2)}, u32[]{:S(2)}) %all-to-all-start.1) | async-done | bytes 589856 | tf_op jit(solution)/shard_map/all_to_all | solution.py:190
  532.1 44.4 %collective-permute-done.17 = bf16[2,192,768]{2,1,0:T(8,128)(2,1)S(1)} collective-permute-done((bf16[2,192,768]{2,1,0:T(8,128)(2,1)S(1)}, bf16[2,192,768]{2,1,0:T(8,128)(2,1)S(1)}, u32[]{:S(2)}, u32[]{:S(2)}) %collective-permute-start.17) | collective-permute-done | bytes 589856 | tf_op jit(solution)/shard_map/ppermute | solution.py:37
  578.2 13.9 %collective-permute-done.18 = bf16[2,192,768]{2,1,0:T(8,128)(2,1)S(1)} collective-permute-done((bf16[2,192,768]{2,1,0:T(8,128)(2,1)S(1)}, bf16[2,192,768]{2,1,0:T(8,128)(2,1)S(1)}, u32[]{:S(2)}, u32[]{:S(2)}) %collective-permute-start.18) | collective-permute-done | bytes 589856 | tf_op jit(solution)/shard_map/ppermute | solution.py:37
  592.9 3.5 fusion.46
  596.6 15.5 %collective-permute-done.13 = bf16[2,48,3072]{2,1,0:T(8,128)(2,1)S(1)} collective-permute-done((bf16[2,48,3072]{2,1,0:T(8,128)(2,1)S(1)}, bf16[2,48,3072]{2,1,0:T(8,128)(2,1)S(1)}, u32[]{:S(2)}, u32[]{:S(2)}) %collective-permute-start.13) | collective-permute-done | bytes 589856 | tf_op jit(solution)/shard_map/ppermute | solution.py:37
  613.2 4.1 collective-permute-start.1
  622.2 5.5 collective-permute-done.14
  634.0 10.9 %collective-permute-done.15 = bf16[2,48,3072]{2,1,0:T(8,128)(2,1)S(1)} collective-permute-done((bf16[2,48,3072]{2,1,0:T(8,128)(2,1)S(1)}, bf16[2,48,3072]{2,1,0:T(8,128)(2,1)S(1)}, u32[]{:S(2)}, u32[]{:S(2)}) %collective-permute-start.15) | collective-permute-done | bytes 589856 | tf_op jit(solution)/shard_map/ppermute | solution.py:37
  646.2 3.6 collective-permute-done.4
  664.5 6.5 collective-permute-done.11
  (219 shorter events, 105.6 us)
Async XLA Ops:
  7.2 89.5 %all-gather.3.cloned.1.call-start = ((), (), s32[]{:S(2)}) async-start(), calls=%async_computation.4 | async-start | bytes 5222400 | tf_op jit(solution)/shard_map/all_gather | solution.py:133
  9.8 254.8 %all-gather.5.cloned.1.call-start = ((), (), s32[]{:S(2)}) async-start(), calls=%async_computation.5 | async-start | bytes 13369344 | tf_op jit(solution)/shard_map/all_gather | solution.py:161
  115.4 347.5 %reduce-scatter.3.cloned.1.call-start = ((), (), s32[]{:S(2)}) async-start(), calls=%async_computation.6 | async-start | bytes 13369344 | tf_op jit(solution)/shard_map/reduce_scatter | solution.py:179
  291.8 330.5 %reduce-scatter.5.cloned.1.call-start = ((), (), s32[]{:S(2)}) async-start(), calls=%async_computation.7 | async-start | bytes 5222400 | tf_op jit(solution)/shard_map/reduce_scatter | solution.py:218
  492.4 15.0 %collective-permute-start.16 = (bf16[2,192,768]{2,1,0:T(8,128)(2,1)S(1)}, bf16[2,192,768]{2,1,0:T(8,128)(2,1)S(1)}, u32[]{:S(2)}, u32[]{:S(2)}) collective-permute-start(bf16[2,192,768]{2,1,0:T(8,128)(2,1)S(1)} %fusion.23), channel_id=1, source_target_pairs={{0,1},{1,0},{2,3},{3,2},{4,5},{5,4},{6,7},{7,6},{8,9},{9,8},{10,11... | collective-permute-start | bytes 1769480 | tf_op jit(solution)/shard_map/ppermute | solution.py:37
  500.2 29.0 %all-to-all-start.1 = ((bf16[2,768,192]{2,0,1:T(2,128)(2,1)}), bf16[2,768,192]{2,0,1:T(2,128)(2,1)S(1)}, u32[]{:S(2)}, u32[]{:S(2)}) async-start(bf16[2,768,192]{2,0,1:T(2,128)(2,1)} %copy.178), calls=%async_computation.3 | async-start | bytes 1572864 | tf_op jit(solution)/shard_map/all_to_all | solution.py:190
  507.5 69.0 %collective-permute-start.17 = (bf16[2,192,768]{2,1,0:T(8,128)(2,1)S(1)}, bf16[2,192,768]{2,1,0:T(8,128)(2,1)S(1)}, u32[]{:S(2)}, u32[]{:S(2)}) collective-permute-start(bf16[2,192,768]{2,1,0:T(8,128)(2,1)S(1)} %add_convert_fusion.2), channel_id=1, source_target_pairs={{0,2},{1,3},{2,0},{3,1},{4,6},{5,7},{6,4},{7,5},{8,10},{9,11},{10,... | collective-permute-start | bytes 1769480 | tf_op jit(solution)/shard_map/ppermute | solution.py:37
  530.4 47.6 %collective-permute-start.12 = (bf16[2,48,3072]{2,1,0:T(8,128)(2,1)S(1)}, bf16[2,48,3072]{2,1,0:T(8,128)(2,1)S(1)}, u32[]{:S(2)}, u32[]{:S(2)}) collective-permute-start(bf16[2,48,3072]{2,1,0:T(8,128)(2,1)S(1)} %all_to_all.33), channel_id=1, source_target_pairs={{0,1},{1,0},{2,3},{3,2},{4,5},{5,4},{6,7},{7,6},{8,9},{9,8},{10,11... | collective-permute-start | bytes 1769480 | tf_op jit(solution)/shard_map/ppermute | solution.py:37
  576.7 15.4 %collective-permute-start.18 = (bf16[2,192,768]{2,1,0:T(8,128)(2,1)S(1)}, bf16[2,192,768]{2,1,0:T(8,128)(2,1)S(1)}, u32[]{:S(2)}, u32[]{:S(2)}) collective-permute-start(bf16[2,192,768]{2,1,0:T(8,128)(2,1)S(1)} %add_convert_fusion.1), channel_id=1, source_target_pairs={{0,4},{1,5},{2,6},{3,7},{4,0},{5,1},{6,2},{7,3},{8,12},{9,13},{10,... | collective-permute-start | bytes 1769480 | tf_op jit(solution)/shard_map/ppermute | solution.py:37
  578.1 34.0 %collective-permute-start.13 = (bf16[2,48,3072]{2,1,0:T(8,128)(2,1)S(1)}, bf16[2,48,3072]{2,1,0:T(8,128)(2,1)S(1)}, u32[]{:S(2)}, u32[]{:S(2)}) collective-permute-start(bf16[2,48,3072]{2,1,0:T(8,128)(2,1)S(1)} %add_convert_fusion.5), channel_id=1, source_target_pairs={{0,2},{1,3},{2,0},{3,1},{4,6},{5,7},{6,4},{7,5},{8,10},{9,11},{10,... | collective-permute-start | bytes 1769480 | tf_op jit(solution)/shard_map/ppermute | solution.py:37
  592.3 25.0 %collective-permute-start.19 = (bf16[2,192,768]{2,1,0:T(8,128)(2,1)S(1)}, bf16[2,192,768]{2,1,0:T(8,128)(2,1)S(1)}, u32[]{:S(2)}, u32[]{:S(2)}) collective-permute-start(bf16[2,192,768]{2,1,0:T(8,128)(2,1)S(1)} %add_convert_fusion), channel_id=1, source_target_pairs={{0,8},{1,9},{2,10},{3,11},{4,12},{5,13},{6,14},{7,15},{8,0},{9,1},... | collective-permute-start | bytes 1769480 | tf_op jit(solution)/shard_map/ppermute | solution.py:37
  596.5 16.7 %collective-permute-start = (f32[2,768]{1,0:T(2,128)S(1)}, f32[2,768]{1,0:T(2,128)S(1)}, u32[]{:S(2)}, u32[]{:S(2)}) collective-permute-start(f32[2,768]{1,0:T(2,128)S(1)} %pad_maximum_fusion.7), channel_id=1, source_target_pairs={{0,16},{16,0},{32,48},{48,32},{64,80},{80,64},{96,112},{112,96},{1... | collective-permute-start | bytes 18440 | tf_op jit(solution)/shard_map/ppermute | solution.py:37
  612.3 15.4 %collective-permute-start.14 = (bf16[2,48,3072]{2,1,0:T(8,128)(2,1)S(1)}, bf16[2,48,3072]{2,1,0:T(8,128)(2,1)}, u32[]{:S(2)}, u32[]{:S(2)}) collective-permute-start(bf16[2,48,3072]{2,1,0:T(8,128)(2,1)S(1)} %add_convert_fusion.4), channel_id=1, source_target_pairs={{0,4},{1,5},{2,6},{3,7},{4,0},{5,1},{6,2},{7,3},{8,12},{9,13},{10,... | collective-permute-start | bytes 1769480 | tf_op jit(solution)/shard_map/ppermute | solution.py:37
  613.2 7.6 %collective-permute-start.1 = (f32[2,768]{1,0:T(2,128)S(1)}, f32[2,768]{1,0:T(2,128)S(1)}, u32[]{:S(2)}, u32[]{:S(2)}) collective-permute-start(f32[2,768]{1,0:T(2,128)S(1)} %fusion.72), channel_id=1, source_target_pairs={{0,32},{16,48},{32,0},{48,16},{64,96},{80,112},{96,64},{112,80},{1... | collective-permute-start | bytes 18440 | tf_op jit(solution)/shard_map/ppermute | solution.py:37
  620.8 9.0 %collective-permute-start.2 = (f32[2,768]{1,0:T(2,128)S(1)}, f32[2,768]{1,0:T(2,128)S(1)}, u32[]{:S(2)}, u32[]{:S(2)}) collective-permute-start(f32[2,768]{1,0:T(2,128)S(1)} %fusion.102), channel_id=1, source_target_pairs={{0,64},{16,80},{32,96},{48,112},{64,0},{80,16},{96,32},{112,48},{1... | collective-permute-start | bytes 18440 | tf_op jit(solution)/shard_map/ppermute | solution.py:37
  622.2 10.6 %collective-permute-start.8 = (bf16[48,3104]{1,0:T(8,128)(2,1)}, bf16[48,3104]{1,0:T(8,128)(2,1)S(1)}, u32[]{:S(2)}, u32[]{:S(2)}) collective-permute-start(bf16[48,3104]{1,0:T(8,128)(2,1)} %reduce-scatter.5.cloned.1.call-done), channel_id=1, source_target_pairs={{0,1},{1,0},{2,3},{3,2},{4,5},{5,4},{6,7},{7,6},{8,9},{9,8},{10,11... | collective-permute-start | bytes 893960 | tf_op jit(solution)/shard_map/ppermute | solution.py:37
  628.9 16.0 %collective-permute-start.15 = (bf16[2,48,3072]{2,1,0:T(8,128)(2,1)S(1)}, bf16[2,48,3072]{2,1,0:T(8,128)(2,1)S(1)}, u32[]{:S(2)}, u32[]{:S(2)}) collective-permute-start(bf16[2,48,3072]{2,1,0:T(8,128)(2,1)S(1)} %add_convert_fusion.3), channel_id=1, source_target_pairs={{0,8},{1,9},{2,10},{3,11},{4,12},{5,13},{6,14},{7,15},{8,0},{9,1},... | collective-permute-start | bytes 1769480 | tf_op jit(solution)/shard_map/ppermute | solution.py:37
  629.9 16.2 %collective-permute-start.3 = (f32[2,768]{1,0:T(2,128)S(1)}, f32[2,768]{1,0:T(2,128)S(1)}, u32[]{:S(2)}, u32[]{:S(2)}) collective-permute-start(f32[2,768]{1,0:T(2,128)S(1)} %add.121), channel_id=1, source_target_pairs={{0,128},{16,144},{32,160},{48,176},{64,192},{80,208},{96,224},{112... | collective-permute-start | bytes 18440 | tf_op jit(solution)/shard_map/ppermute | solution.py:37
  633.9 17.0 %collective-permute-start.9 = (bf16[48,3104]{1,0:T(8,128)(2,1)S(1)}, bf16[48,3104]{1,0:T(8,128)(2,1)S(1)}, u32[]{:S(2)}, u32[]{:S(2)}) collective-permute-start(bf16[48,3104]{1,0:T(8,128)(2,1)S(1)} %add_convert_fusion.8), channel_id=1, source_target_pairs={{0,2},{1,3},{2,0},{3,1},{4,6},{5,7},{6,4},{7,5},{8,10},{9,11},{10,... | collective-permute-start | bytes 893960 | tf_op jit(solution)/shard_map/ppermute | solution.py:37
  649.8 4.5 collective-permute-start.5
  650.9 10.5 %collective-permute-start.10 = (bf16[48,3104]{1,0:T(8,128)(2,1)S(1)}, bf16[48,3104]{1,0:T(8,128)(2,1)S(1)}, u32[]{:S(2)}, u32[]{:S(2)}) collective-permute-start(bf16[48,3104]{1,0:T(8,128)(2,1)S(1)} %add_convert_fusion.7), channel_id=1, source_target_pairs={{0,4},{1,5},{2,6},{3,7},{4,0},{5,1},{6,2},{7,3},{8,12},{9,13},{10,... | collective-permute-start | bytes 893960 | tf_op jit(solution)/shard_map/ppermute | solution.py:37
  654.3 4.4 collective-permute-start.6
  658.7 5.1 collective-permute-start.7
  661.5 9.5 %collective-permute-start.11 = (bf16[48,3104]{1,0:T(8,128)(2,1)S(1)}, bf16[48,3104]{1,0:T(8,128)(2,1)S(1)}, u32[]{:S(2)}, u32[]{:S(2)}) collective-permute-start(bf16[48,3104]{1,0:T(8,128)(2,1)S(1)} %add_convert_fusion.6), channel_id=1, source_target_pairs={{0,8},{1,9},{2,10},{3,11},{4,12},{5,13},{6,14},{7,15},{8,0},{9,1},... | collective-permute-start | bytes 893960 | tf_op jit(solution)/shard_map/ppermute | solution.py:37
  (35 other events, 929.6 us)
Sparse Core Ops, SparseCore 0:
  11.2 85.3 all-gather.2
  115.5 149.0 all-gather.4
  291.9 170.9 reduce-scatter.2
  486.8 124.1 reduce-scatter.4
where the time goes:
time: 687 us; the launch traced here: 680 us
  waiting for transfers between devices  476 us (69%)
  matrix products  49.8 us (7%)
  blocking collectives  39.2 us (6%)
  other arithmetic  37.6 us (5%)
  local copies, waits for them, and re-layouts  35.7 us (5%)
  starting transfers between devices  27.2 us (4%)
  between operations  14.8 us (2%)
    reduce_scatter x1, waiting for transfers between devices, body(): lax.psum_scatter(jnp.stack([out_part, rows_part]), 'shard', scatter_dimen...  171 us
    ppermute x20, waiting for transfers between devices, butterfly_sum(): other = lax.ppermute(sent, axis, pairs)  111 us
    all_gather x1, waiting for transfers between devices, body(): lax.all_gather(jnp.stack([expert_rows, grad_eout]), 'shard', axis=2, tile...  93.5 us
    all_gather x1, waiting for transfers between devices, body(): lax.all_gather(jnp.concatenate([w_qkv, w_proj, w_router], axis=1), 'shard...  79 us
    all_to_all x1, blocking collectives, body(): w_in_cols = lax.all_to_all(w_expert_in, 'shard', 2, 1, tiled=True)  39.2 us
    ppermute x20, starting transfers between devices, butterfly_sum(): other = lax.ppermute(sent, axis, pairs)  23.2 us
    all_to_all x1, waiting for transfers between devices, body(): lax.all_to_all(gin_cols.astype(jnp.bfloat16), 'shard', 1, 2, tiled=True)  20.7 us
    unnamed x74, local copies, waits for them, and re-layouts  16.6 us
  transfers between devices with their start and end apart: 25, of which 16 were waited for; matrix products, arithmetic and copies ran while one was open for 7% of the time, Pallas kernels for 0%

commit v1 on v0

--- a/solution.py
+++ b/solution.py
@@ -158,7 +158,12 @@
     w_in_cols = lax.all_to_all(w_expert_in, "shard", 2, 1, tiled=True)
     grad = cotangent.astype(jnp.float32)
     grad_eout = jnp.einsum("rec,rd->ecd", combine, grad, precision=high).astype(jnp.bfloat16)
-    gathered = lax.all_gather(jnp.stack([expert_rows, grad_eout]), "shard", axis=2, tiled=True)
+    gathered = jnp.concatenate(
+        lax.all_to_all(
+            jnp.stack(lax.axis_size("shard") * [jnp.stack([expert_rows, grad_eout])]), "shard", 0, 0
+        ),
+        axis=2,
+    )
     rows_all, geout_all = (gathered[0], gathered[1])
     pre = jnp.einsum("erd,edh->erh", rows_all, w_in_cols, preferred_element_type=jnp.float32)
     activated = jax.nn.gelu(pre, approximate=False).astype(jnp.bfloat16)

time: 687 us -> 859 us (1.25)
  waiting for transfers between devices: 476 us -> 654 us
  blocking collectives: 39.2 us -> 0 us
  starting transfers between devices: 27.2 us -> 47.4 us
  local copies, waits for them, and re-layouts: 35.7 us -> 51.6 us
    all_to_all x0 -> x2, waiting for transfers between devices: none -> 280 us  [the longest x1 280 us: body(): lax.all_to_all(jnp.stack(lax.axis_size('shard') * [jnp.stack([expert_rows...]
    all_gather x1 -> x0, waiting for transfers between devices: 93.5 us -> none  [body(): lax.all_gather(jnp.stack([expert_rows, grad_eout]), 'shard', axis=2, tile...]
    all_to_all x1 -> x0, blocking collectives: 39.2 us -> none  [body(): w_in_cols = lax.all_to_all(w_expert_in, 'shard', 2, 1, tiled=True)]
    all_to_all x0 -> x2, starting transfers between devices: none -> 16.2 us  [the longest x1 11.2 us: body(): w_in_cols = lax.all_to_all(w_expert_in, 'shard', 2, 1, tiled=True)]
    slice x1 -> x4, local copies, waits for them, and re-layouts: 0.21 us -> 9.42 us  [the longest x3 9.21 us: body(): rows_all, geout_all = (gathered[0], gathered[1])]
  transfers between devices with their start and end apart: 25 -> 26, of which waited for: 16 -> 17; matrix products, arithmetic and copies ran while one was open for 7% -> 7% of each run, Pallas kernels for 0% -> 0%
where the time goes in v1:
time: 859 us; the launch traced here: 849 us
  waiting for transfers between devices  654 us (76%)
  local copies, waits for them, and re-layouts  51.6 us (6%)
  starting transfers between devices  47.4 us (6%)
  matrix products  46.3 us (5%)
  other arithmetic  35.6 us (4%)
  between operations  15 us (2%)
    all_to_all x1, waiting for transfers between devices, body(): lax.all_to_all(jnp.stack(lax.axis_size('shard') * [jnp.stack([expert_rows...  280 us
    reduce_scatter x1, waiting for transfers between devices, body(): lax.psum_scatter(jnp.stack([out_part, rows_part]), 'shard', scatter_dimen...  176 us
    ppermute x20, waiting for transfers between devices, butterfly_sum(): other = lax.ppermute(sent, axis, pairs)  107 us
    all_gather x1, waiting for transfers between devices, body(): lax.all_gather(jnp.concatenate([w_qkv, w_proj, w_router], axis=1), 'shard...  74 us
    ppermute x20, starting transfers between devices, butterfly_sum(): other = lax.ppermute(sent, axis, pairs)  26.8 us
  transfers between devices with their start and end apart: 26, of which 17 were waited for; matrix products, arithmetic and copies ran while one was open for 7% of the time, Pallas kernels for 0%

profile of v1, /device:TPU:4, one launch (start us, length us, event | category | flops | bytes accessed | tf_op | source)
XLA Modules:
  0.0 849.4 jit_solution(2476435747398327314)
XLA Ops:
  9.8 3.7 copy.167
  16.6 11.2 %all-to-all-start.1 = ((bf16[16,2,9216]{2,1,0:T(2,128)(2,1)}), bf16[16,2,9216]{2,1,0:T(2,128)(2,1)}, u32[]{:S(2)}, u32[]{:S(2)}) async-start(bf16[16,2,9216]{2,1,0:T(2,128)(2,1)} %reshape.260), calls=%async_computation.1 | async-start | bytes 1179648 | tf_op jit(solution)/shard_map/all_to_all | solution.py:158
  31.7 74.0 %all-gather.2.cloned.1.call-done = bf16[768,3104]{1,0:T(8,128)(2,1)} async-done(((bf16[48,3104]{1,0:T(8,128)(2,1)}), bf16[768,3104]{1,0:T(8,128)(2,1)}) %all-gather.2.cloned.1.call-update) | async-done | bytes 4767760 | tf_op jit(solution)/shard_map/all_gather | solution.py:133
  124.3 7.1 stack.23
  131.4 4.9 all-to-all-start
  140.2 4.7 copy.168
  144.9 280.2 %all-to-all-done = bf16[16,2,2,128,768]{4,3,2,1,0:T(8,128)(2,1)} async-done(((bf16[16,2,2,128,768]{4,3,2,1,0:T(8,128)(2,1)}), bf16[16,2,2,128,768]{4,3,2,1,0:T(8,128)(2,1)}, u32[]{:S(2)}, u32[]{:S(2)}) %all-to-all-start) | async-done | bytes 12582944 | tf_op jit(solution)/shard_map/all_to_all | solution.py:162
  425.1 5.6 fusion.69
  434.8 4.5 fusion.28
  440.5 4.0 fusion.8
  447.0 7.2 fusion.2
  456.1 5.7 pad_maximum_fusion
  462.1 175.9 %reduce-scatter.3.cloned.1.call-done = bf16[2,2,128,768]{3,2,1,0:T(8,128)(2,1)} async-done(((bf16[2,2,2048,768]{3,2,1,0:T(8,128)(2,1)}), bf16[2,2,128,768]{3,2,1,0:T(8,128)(2,1)}) %reduce-scatter.3.cloned.1.call-update) | async-done | bytes 786448 | tf_op jit(solution)/shard_map/reduce_scatter | solution.py:184
  661.9 4.8 convolution_convert_fusion.4
  673.7 3.6 all-to-all-start.2
  677.3 8.1 collective-permute-done.16
  686.9 16.4 %all-to-all-done.2 = bf16[2,768,192]{2,0,1:T(2,128)(2,1)S(1)} async-done(((bf16[2,768,192]{2,0,1:T(2,128)(2,1)}), bf16[2,768,192]{2,0,1:T(2,128)(2,1)S(1)}, u32[]{:S(2)}, u32[]{:S(2)}) %all-to-all-start.2) | async-done | bytes 589856 | tf_op jit(solution)/shard_map/all_to_all | solution.py:195
  705.6 44.9 %collective-permute-done.17 = bf16[2,192,768]{2,1,0:T(8,128)(2,1)S(1)} collective-permute-done((bf16[2,192,768]{2,1,0:T(8,128)(2,1)S(1)}, bf16[2,192,768]{2,1,0:T(8,128)(2,1)S(1)}, u32[]{:S(2)}, u32[]{:S(2)}) %collective-permute-start.17) | collective-permute-done | bytes 589856 | tf_op jit(solution)/shard_map/ppermute | solution.py:37
  752.3 13.8 %collective-permute-done.18 = bf16[2,192,768]{2,1,0:T(8,128)(2,1)S(1)} collective-permute-done((bf16[2,192,768]{2,1,0:T(8,128)(2,1)S(1)}, bf16[2,192,768]{2,1,0:T(8,128)(2,1)S(1)}, u32[]{:S(2)}, u32[]{:S(2)}) %collective-permute-start.18) | collective-permute-done | bytes 589856 | tf_op jit(solution)/shard_map/ppermute | solution.py:37
  770.6 13.4 %collective-permute-done.13 = bf16[2,48,3072]{2,1,0:T(8,128)(2,1)S(1)} collective-permute-done((bf16[2,48,3072]{2,1,0:T(8,128)(2,1)S(1)}, bf16[2,48,3072]{2,1,0:T(8,128)(2,1)S(1)}, u32[]{:S(2)}, u32[]{:S(2)}) %collective-permute-start.13) | collective-permute-done | bytes 589856 | tf_op jit(solution)/shard_map/ppermute | solution.py:37
  793.9 5.4 collective-permute-start.8
  809.6 7.2 collective-permute-done.15
  818.1 4.4 collective-permute-done.4
  836.7 3.7 collective-permute-done.11
  (258 shorter events, 119.9 us)
Async XLA Ops:
  7.2 98.4 %all-gather.2.cloned.1.call-start = ((), (), s32[]{:S(2)}) async-start(), calls=%async_computation.5 | async-start | bytes 5222400 | tf_op jit(solution)/shard_map/all_gather | solution.py:133
  16.6 107.6 %all-to-all-start.1 = ((bf16[16,2,9216]{2,1,0:T(2,128)(2,1)}), bf16[16,2,9216]{2,1,0:T(2,128)(2,1)}, u32[]{:S(2)}, u32[]{:S(2)}) async-start(bf16[16,2,9216]{2,1,0:T(2,128)(2,1)} %reshape.260), calls=%async_computation.1 | async-start | bytes 1179648 | tf_op jit(solution)/shard_map/all_to_all | solution.py:158
  131.4 293.7 %all-to-all-start = ((bf16[16,2,2,128,768]{4,3,2,1,0:T(8,128)(2,1)}), bf16[16,2,2,128,768]{4,3,2,1,0:T(8,128)(2,1)}, u32[]{:S(2)}, u32[]{:S(2)}) async-start(bf16[16,2,2,128,768]{4,3,2,1,0:T(8,128)(2,1)} %stack.23), calls=%async_computation | async-start | bytes 25165824 | tf_op jit(solution)/shard_map/all_to_all | solution.py:162
  136.3 501.7 %reduce-scatter.3.cloned.1.call-start = ((), (), s32[]{:S(2)}) async-start(), calls=%async_computation.6 | async-start | bytes 13369344 | tf_op jit(solution)/shard_map/reduce_scatter | solution.py:184
  461.9 332.1 %reduce-scatter.5.cloned.1.call-start = ((), (), s32[]{:S(2)}) async-start(), calls=%async_computation.7 | async-start | bytes 5222400 | tf_op jit(solution)/shard_map/reduce_scatter | solution.py:223
  666.8 18.7 %collective-permute-start.16 = (bf16[2,192,768]{2,1,0:T(8,128)(2,1)S(1)}, bf16[2,192,768]{2,1,0:T(8,128)(2,1)}, u32[]{:S(2)}, u32[]{:S(2)}) collective-permute-start(bf16[2,192,768]{2,1,0:T(8,128)(2,1)S(1)} %convolution_convert_fusion.4), channel_id=1, source_target_pairs={{0,1},{1,0},{2,3},{3,2},{4,5},{5,4},{6,7},{7,6},{8,9},{9,8},{10,11... | collective-permute-start | bytes 1769480 | tf_op jit(solution)/shard_map/ppermute | solution.py:37
  673.7 29.6 %all-to-all-start.2 = ((bf16[2,768,192]{2,0,1:T(2,128)(2,1)}), bf16[2,768,192]{2,0,1:T(2,128)(2,1)S(1)}, u32[]{:S(2)}, u32[]{:S(2)}) async-start(bf16[2,768,192]{2,0,1:T(2,128)(2,1)} %copy.184), calls=%async_computation.4 | async-start | bytes 1572864 | tf_op jit(solution)/shard_map/all_to_all | solution.py:195
  686.8 63.7 %collective-permute-start.17 = (bf16[2,192,768]{2,1,0:T(8,128)(2,1)S(1)}, bf16[2,192,768]{2,1,0:T(8,128)(2,1)S(1)}, u32[]{:S(2)}, u32[]{:S(2)}) collective-permute-start(bf16[2,192,768]{2,1,0:T(8,128)(2,1)S(1)} %add_convert_fusion.2), channel_id=1, source_target_pairs={{0,2},{1,3},{2,0},{3,1},{4,6},{5,7},{6,4},{7,5},{8,10},{9,11},{10,... | collective-permute-start | bytes 1769480 | tf_op jit(solution)/shard_map/ppermute | solution.py:37
  704.5 47.5 %collective-permute-start.12 = (bf16[2,48,3072]{2,1,0:T(8,128)(2,1)S(1)}, bf16[2,48,3072]{2,1,0:T(8,128)(2,1)S(1)}, u32[]{:S(2)}, u32[]{:S(2)}) collective-permute-start(bf16[2,48,3072]{2,1,0:T(8,128)(2,1)S(1)} %all_to_all.37), channel_id=1, source_target_pairs={{0,1},{1,0},{2,3},{3,2},{4,5},{5,4},{6,7},{7,6},{8,9},{9,8},{10,11... | collective-permute-start | bytes 1769480 | tf_op jit(solution)/shard_map/ppermute | solution.py:37
  750.7 15.4 %collective-permute-start.18 = (bf16[2,192,768]{2,1,0:T(8,128)(2,1)S(1)}, bf16[2,192,768]{2,1,0:T(8,128)(2,1)S(1)}, u32[]{:S(2)}, u32[]{:S(2)}) collective-permute-start(bf16[2,192,768]{2,1,0:T(8,128)(2,1)S(1)} %add_convert_fusion.1), channel_id=1, source_target_pairs={{0,4},{1,5},{2,6},{3,7},{4,0},{5,1},{6,2},{7,3},{8,12},{9,13},{10,... | collective-permute-start | bytes 1769480 | tf_op jit(solution)/shard_map/ppermute | solution.py:37
  752.2 31.8 %collective-permute-start.13 = (bf16[2,48,3072]{2,1,0:T(8,128)(2,1)S(1)}, bf16[2,48,3072]{2,1,0:T(8,128)(2,1)S(1)}, u32[]{:S(2)}, u32[]{:S(2)}) collective-permute-start(bf16[2,48,3072]{2,1,0:T(8,128)(2,1)S(1)} %add_convert_fusion.5), channel_id=1, source_target_pairs={{0,2},{1,3},{2,0},{3,1},{4,6},{5,7},{6,4},{7,5},{8,10},{9,11},{10,... | collective-permute-start | bytes 1769480 | tf_op jit(solution)/shard_map/ppermute | solution.py:37
  766.2 22.3 %collective-permute-start.19 = (bf16[2,192,768]{2,1,0:T(8,128)(2,1)S(1)}, bf16[2,192,768]{2,1,0:T(8,128)(2,1)S(1)}, u32[]{:S(2)}, u32[]{:S(2)}) collective-permute-start(bf16[2,192,768]{2,1,0:T(8,128)(2,1)S(1)} %add_convert_fusion), channel_id=1, source_target_pairs={{0,8},{1,9},{2,10},{3,11},{4,12},{5,13},{6,14},{7,15},{8,0},{9,1},... | collective-permute-start | bytes 1769480 | tf_op jit(solution)/shard_map/ppermute | solution.py:37
  770.5 14.6 %collective-permute-start = (f32[2,768]{1,0:T(2,128)S(1)}, f32[2,768]{1,0:T(2,128)S(1)}, u32[]{:S(2)}, u32[]{:S(2)}) collective-permute-start(f32[2,768]{1,0:T(2,128)S(1)} %pad_maximum_fusion.7), channel_id=1, source_target_pairs={{0,16},{16,0},{32,48},{48,32},{64,80},{80,64},{96,112},{112,96},{1... | collective-permute-start | bytes 18440 | tf_op jit(solution)/shard_map/ppermute | solution.py:37
  784.1 15.4 %collective-permute-start.14 = (bf16[2,48,3072]{2,1,0:T(8,128)(2,1)S(1)}, bf16[2,48,3072]{2,1,0:T(8,128)(2,1)}, u32[]{:S(2)}, u32[]{:S(2)}) collective-permute-start(bf16[2,48,3072]{2,1,0:T(8,128)(2,1)S(1)} %add_convert_fusion.4), channel_id=1, source_target_pairs={{0,4},{1,5},{2,6},{3,7},{4,0},{5,1},{6,2},{7,3},{8,12},{9,13},{10,... | collective-permute-start | bytes 1769480 | tf_op jit(solution)/shard_map/ppermute | solution.py:37
  785.1 7.6 collective-permute-start.1
  792.7 8.9 %collective-permute-start.2 = (f32[2,768]{1,0:T(2,128)S(1)}, f32[2,768]{1,0:T(2,128)S(1)}, u32[]{:S(2)}, u32[]{:S(2)}) collective-permute-start(f32[2,768]{1,0:T(2,128)S(1)} %fusion.101), channel_id=1, source_target_pairs={{0,64},{16,80},{32,96},{48,112},{64,0},{80,16},{96,32},{112,48},{1... | collective-permute-start | bytes 18440 | tf_op jit(solution)/shard_map/ppermute | solution.py:37
  793.9 12.1 %collective-permute-start.8 = (bf16[48,3104]{1,0:T(8,128)(2,1)}, bf16[48,3104]{1,0:T(8,128)(2,1)S(1)}, u32[]{:S(2)}, u32[]{:S(2)}) collective-permute-start(bf16[48,3104]{1,0:T(8,128)(2,1)} %reduce-scatter.5.cloned.1.call-done), channel_id=1, source_target_pairs={{0,1},{1,0},{2,3},{3,2},{4,5},{5,4},{6,7},{7,6},{8,9},{9,8},{10,11... | collective-permute-start | bytes 893960 | tf_op jit(solution)/shard_map/ppermute | solution.py:37
  800.8 16.0 %collective-permute-start.15 = (bf16[2,48,3072]{2,1,0:T(8,128)(2,1)S(1)}, bf16[2,48,3072]{2,1,0:T(8,128)(2,1)S(1)}, u32[]{:S(2)}, u32[]{:S(2)}) collective-permute-start(bf16[2,48,3072]{2,1,0:T(8,128)(2,1)S(1)} %add_convert_fusion.3), channel_id=1, source_target_pairs={{0,8},{1,9},{2,10},{3,11},{4,12},{5,13},{6,14},{7,15},{8,0},{9,1},... | collective-permute-start | bytes 1769480 | tf_op jit(solution)/shard_map/ppermute | solution.py:37
  801.6 16.3 %collective-permute-start.3 = (f32[2,768]{1,0:T(2,128)S(1)}, f32[2,768]{1,0:T(2,128)S(1)}, u32[]{:S(2)}, u32[]{:S(2)}) collective-permute-start(f32[2,768]{1,0:T(2,128)S(1)} %add.121), channel_id=1, source_target_pairs={{0,128},{16,144},{32,160},{48,176},{64,192},{80,208},{96,224},{112... | collective-permute-start | bytes 18440 | tf_op jit(solution)/shard_map/ppermute | solution.py:37
  807.1 15.3 %collective-permute-start.9 = (bf16[48,3104]{1,0:T(8,128)(2,1)S(1)}, bf16[48,3104]{1,0:T(8,128)(2,1)S(1)}, u32[]{:S(2)}, u32[]{:S(2)}) collective-permute-start(bf16[48,3104]{1,0:T(8,128)(2,1)S(1)} %add_convert_fusion.8), channel_id=1, source_target_pairs={{0,2},{1,3},{2,0},{3,1},{4,6},{5,7},{6,4},{7,5},{8,10},{9,11},{10,... | collective-permute-start | bytes 893960 | tf_op jit(solution)/shard_map/ppermute | solution.py:37
  822.4 4.5 collective-permute-start.5
  822.5 9.3 %collective-permute-start.10 = (bf16[48,3104]{1,0:T(8,128)(2,1)S(1)}, bf16[48,3104]{1,0:T(8,128)(2,1)S(1)}, u32[]{:S(2)}, u32[]{:S(2)}) collective-permute-start(bf16[48,3104]{1,0:T(8,128)(2,1)S(1)} %add_convert_fusion.7), channel_id=1, source_target_pairs={{0,4},{1,5},{2,6},{3,7},{4,0},{5,1},{6,2},{7,3},{8,12},{9,13},{10,... | collective-permute-start | bytes 893960 | tf_op jit(solution)/shard_map/ppermute | solution.py:37
  830.9 5.3 collective-permute-start.7
  831.9 8.6 %collective-permute-start.11 = (bf16[48,3104]{1,0:T(8,128)(2,1)S(1)}, bf16[48,3104]{1,0:T(8,128)(2,1)S(1)}, u32[]{:S(2)}, u32[]{:S(2)}) collective-permute-start(bf16[48,3104]{1,0:T(8,128)(2,1)S(1)} %add_convert_fusion.6), channel_id=1, source_target_pairs={{0,8},{1,9},{2,10},{3,11},{4,12},{5,13},{6,14},{7,15},{8,0},{9,1},... | collective-permute-start | bytes 893960 | tf_op jit(solution)/shard_map/ppermute | solution.py:37
  (53 other events, 1996.4 us)
Sparse Core Ops, SparseCore 0:
  11.2 94.3 all-gather.1
  461.9 176.0 reduce-scatter.2
  662.0 127.3 reduce-scatter.4
